TPU v7x, 32 devices: a whole 2x2x4 slice. The times are simulated.
32 devices in a mesh: crop: 1, res: 32 (over z, y, x, core).
Axes of the slice: x: 2, y: 2, z: 4, core: 2. Of those that a mesh axis runs over, the one named last changes fastest.
Arguments:
- homolog_symbol_ids: int32 [64, 128], P(('crop', 'res')), may hold values from 0 to 22
- residue_attend_mask: int32 [128], P('crop'), may hold values 0 or 1
- alignment_state: bfloat16 [64, 128, 256], P(('crop', 'res')), may hold values from -6 to 6
- pair: bfloat16 [128, 128, 128], P(('crop', 'res')), may hold values from -6 to 6
- symbol_lookup_matrix: bfloat16 [23, 256], replicated, may hold values from -3 to 3
- pair_bias_weight: bfloat16 [128, 8], replicated, may hold values from -0.5 to 0.5
- row_projection_weight: bfloat16 [256, 1024], replicated, may hold values from -8 to 8
- horizontal_readout_matrix: bfloat16 [256, 256], replicated, may hold values from -0.375 to 0.375
- column_projection_weight: bfloat16 [256, 1024], replicated, may hold values from -8 to 8
- vertical_readout_matrix: bfloat16 [256, 256], replicated, may hold values from -0.375 to 0.375
- product_factor_matrices: bfloat16 [256, 64], replicated, may hold values from -0.375 to 0.375
- outer_output_weight: bfloat16 [1024, 128], replicated, may hold values from -1.5 to 1.5
- triangle_input_weight: bfloat16 [128, 640], replicated, may hold values from -0.5 to 0.5
- triangle_output_weight: bfloat16 [128, 128], replicated, may hold values from -0.5 to 0.5
Outputs:
- alignment_output: bfloat16 [64, 128, 256], P('crop', 'res')
- pair_output: bfloat16 [128, 128, 128], P(('crop', 'res'))
All inputs are finite; a program needn't handle non-finite values.
Results may differ from a plain program's by a relative error of at most 0.013.
Values may be sent and summed in bfloat16 or wider, within the bound.
A program may use at most 64 MiB of HBM per device.

v0:
```python
import jax
import jax.numpy as jnp
from jax import lax
from jax.sharding import PartitionSpec as P

EPSILON = 1e-05


def layer_normalized(input_rows, axis):
    average = jnp.mean(input_rows, axis, keepdims=True)
    centred = input_rows - average
    spread = jnp.mean(centred * centred, axis, keepdims=True)
    return centred * lax.rsqrt(spread + EPSILON)


def split_proj(input_rows, weight, head_count):
    channels = weight.shape[0]
    head_size = channels // head_count
    projected = jnp.einsum("blc,ce->ble", input_rows, weight, preferred_element_type=jnp.float32)
    lead = projected.shape[:2]
    query_tensor = (
        (projected[..., :channels] * head_size ** (-0.5))
        .astype(jnp.bfloat16)
        .reshape(lead + (head_count, head_size))
    )
    key_tensor = (
        projected[..., channels : 2 * channels]
        .astype(jnp.bfloat16)
        .reshape(lead + (head_count, head_size))
    )
    value_tensor = (
        projected[..., 2 * channels : 3 * channels]
        .astype(jnp.bfloat16)
        .reshape(lead + (head_count, head_size))
    )
    gate_values = projected[..., 3 * channels :]
    return (query_tensor, key_tensor, value_tensor, gate_values)


def attention_block_fn(query_tensor, key_tensor, value_tensor, gate_values, extra_bias, out_weight):
    scores = (
        jnp.einsum("bqhd,bkhd->bhqk", query_tensor, key_tensor, preferred_element_type=jnp.float32)
        + extra_bias
    )
    row_top = jnp.max(scores, -1, keepdims=True)
    exp_scores = jnp.exp(scores - row_top)
    weights = (exp_scores / jnp.sum(exp_scores, -1, keepdims=True)).astype(jnp.bfloat16)
    mixed = jnp.einsum("bhqk,bkhd->bqhd", weights, value_tensor, preferred_element_type=jnp.float32)
    gated = (jax.nn.sigmoid(gate_values) * mixed.reshape(gate_values.shape)).astype(jnp.bfloat16)
    return jnp.einsum("bqc,ce->bqe", gated, out_weight, preferred_element_type=jnp.float32)


def shards(
    homolog_symbol_ids,
    residue_attend_mask,
    alignment_state,
    pair,
    symbol_lookup_matrix,
    pair_bias_weight,
    row_projection_weight,
    horizontal_readout_matrix,
    column_projection_weight,
    vertical_readout_matrix,
    product_factor_matrices,
    outer_output_weight,
    triangle_input_weight,
    triangle_output_weight,
):
    residue_count = lax.axis_size("res")
    sequence_total = alignment_state.shape[0] * residue_count
    res_local = pair.shape[0]
    chain_total = pair.shape[1]
    pair_chan = pair.shape[2]
    owner_chan = pair_chan // residue_count
    outer_chan = product_factor_matrices.shape[1] // 2
    head_count = pair_bias_weight.shape[1]
    token_class_count = symbol_lookup_matrix.shape[0]
    one_hot_tokens = (
        homolog_symbol_ids[:, :, None]
        == jnp.arange(token_class_count, dtype=jnp.int32)[None, None, :]
    ).astype(jnp.bfloat16)
    alignment_initial = alignment_state.astype(jnp.float32) + jnp.einsum(
        "kly,yb->klb", one_hot_tokens, symbol_lookup_matrix, preferred_element_type=jnp.float32
    )
    pair_normed = layer_normalized(pair.astype(jnp.float32), -1).astype(jnp.bfloat16)
    bias_local = jnp.einsum(
        "ijc,ch->hij", pair_normed, pair_bias_weight, preferred_element_type=jnp.float32
    ).astype(jnp.bfloat16)
    mask_bias = (residue_attend_mask.astype(jnp.float32) - 1.0) * 10000.0
    row_input = layer_normalized(alignment_initial, -1).astype(jnp.bfloat16)
    query_tensor, key_tensor, value_tensor, gate_values = split_proj(
        row_input, row_projection_weight, head_count
    )
    bias_all = lax.all_gather(bias_local, "res", axis=1, tiled=True)
    extra_bias = bias_all.astype(jnp.float32)[None] + mask_bias[None, None, None, :]
    row_attention_update = attention_block_fn(
        query_tensor, key_tensor, value_tensor, gate_values, extra_bias, horizontal_readout_matrix
    )
    alignment_after_rows = (alignment_initial + row_attention_update).astype(jnp.bfloat16)
    alignment_columns = lax.all_to_all(
        alignment_after_rows, "res", split_axis=1, concat_axis=0, tiled=True
    )
    column_start = jnp.swapaxes(alignment_columns, 0, 1).astype(jnp.float32)
    col_in = layer_normalized(column_start, -1).astype(jnp.bfloat16)
    col_queries, col_keys, col_values, col_gating = split_proj(
        col_in, column_projection_weight, head_count
    )
    alignment_after_columns = column_start + attention_block_fn(
        col_queries, col_keys, col_values, col_gating, jnp.float32(0.0), vertical_readout_matrix
    )
    alignment_output = jnp.swapaxes(alignment_after_columns, 0, 1).astype(jnp.bfloat16)
    outer_input = layer_normalized(alignment_after_columns, -1).astype(jnp.bfloat16)
    factor_ab = jnp.einsum(
        "rsc,ce->rse", outer_input, product_factor_matrices, preferred_element_type=jnp.float32
    )
    left = factor_ab[..., :outer_chan].astype(jnp.bfloat16)
    latter_factor = (
        factor_ab[..., outer_chan:]
        .astype(jnp.bfloat16)
        .reshape(res_local, sequence_total * outer_chan)
    )
    piece = lax.all_gather(latter_factor, "res", axis=0, tiled=True)
    count = piece.shape[0]
    right_rows = piece.reshape(count, sequence_total, outer_chan)
    cross_product_result = (
        jnp.einsum("isc,jsd->ijcd", left, right_rows, preferred_element_type=jnp.float32)
        / sequence_total
    ).astype(jnp.bfloat16)
    update = jnp.einsum(
        "ije,ez->ijz",
        cross_product_result.reshape(res_local, count, outer_chan * outer_chan),
        outer_output_weight,
        preferred_element_type=jnp.float32,
    )
    pair_one = pair.astype(jnp.float32) + update
    tri_normed = layer_normalized(pair_one, -1).astype(jnp.bfloat16)
    factors = jnp.einsum(
        "ijc,ce->eij",
        tri_normed,
        triangle_input_weight[:, : 4 * pair_chan],
        preferred_element_type=jnp.float32,
    )
    gate_out = jnp.einsum(
        "ijc,ce->ije",
        tri_normed,
        triangle_input_weight[:, 4 * pair_chan :],
        preferred_element_type=jnp.float32,
    )
    left_f = (jax.nn.sigmoid(factors[pair_chan : 2 * pair_chan]) * factors[:pair_chan]).astype(
        jnp.bfloat16
    )
    right_f = (
        jax.nn.sigmoid(factors[3 * pair_chan :]) * factors[2 * pair_chan : 3 * pair_chan]
    ).astype(jnp.bfloat16)
    left_f = left_f.reshape(residue_count, owner_chan, res_local, chain_total)
    right_f = right_f.reshape(residue_count, owner_chan, res_local, chain_total)
    combined = jnp.einsum(
        "xcik,xcjk->xcij",
        lax.all_to_all(left_f, "res", split_axis=0, concat_axis=2, tiled=True),
        lax.all_to_all(right_f, "res", split_axis=0, concat_axis=2, tiled=True),
        preferred_element_type=jnp.float32,
    ).astype(jnp.bfloat16)
    back_rows = lax.all_to_all(combined, "res", split_axis=2, concat_axis=0, tiled=True)
    back_rows = back_rows.reshape(pair_chan, res_local, chain_total)
    comb_normed = layer_normalized(back_rows.astype(jnp.float32), 0).astype(jnp.bfloat16)
    tri_update = jnp.einsum(
        "cij,cz->ijz", comb_normed, triangle_output_weight, preferred_element_type=jnp.float32
    )
    pair_output = (pair_one + jax.nn.sigmoid(gate_out) * tri_update).astype(jnp.bfloat16)
    return (alignment_output, pair_output)


def solution(mesh):
    placed = (
        P(("crop", "res"), None),
        P("crop"),
        P(("crop", "res"), None, None),
        P(("crop", "res"), None, None),
        P(),
        P(),
        P(),
        P(),
        P(),
        P(),
        P(),
        P(),
        P(),
        P(),
    )
    return jax.shard_map(
        shards,
        mesh=mesh,
        in_specs=placed,
        out_specs=(P("crop", "res", None), P(("crop", "res"), None, None)),
        check_vma=False,
    )
```

profile of v0, /device:TPU:0, one launch (start us, length us, event | category | flops | bytes accessed | tf_op | source)
XLA Modules:
  0.0 155.3 jit_solution(11216174859262117624)
XLA Ops:
  0.7 0.7 add_multiply_fusion
  1.4 1.0 copy.74
  2.5 0.8 fusion.14
  3.4 43.9 %all_gather.6 = bf16[8,128,128]{2,0,1:T(8,128)(2,1)S(1)} all-gather(bf16[8,4,128]{2,0,1:T(8,128)(2,1)S(1)} %fusion.14), channel_id=1, replica_groups=mesh['crop'=1,'res'=32] {'res'}, dimensions={1}, use_global_device_ids=true | all-gather | bytes 270336 | tf_op jit(solution)/shard_map/all_gather | solution.py:94
  47.3 0.2 copy.76
  47.6 0.3 fusion.84
  47.9 0.2 multiply_reduce_fusion.3
  48.1 0.3 fusion.85
  48.5 0.7 fusion.83
  49.2 0.1 copy.73
  49.3 0.1 copy.72
  49.5 0.5 copy-done.1
  49.9 0.2 copy-done.2
  50.1 0.5 fusion.86
  50.6 1.3 convolution_add_fusion
  51.9 1.0 copy.71
  53.0 1.0 fusion.20
  54.0 1.1 copy.78
  55.2 1.1 fusion.11
  56.3 0.1 copy.79
  56.4 9.9 %all_to_all.48 = bf16[2,128,256]{2,0,1:T(2,128)(2,1)S(1)} all-to-all(bf16[2,128,256]{2,0,1:T(2,128)(2,1)S(1)} %copy.79), channel_id=1, replica_groups=mesh['crop'=1,'res'=32] {'res'}, dimensions={1} | all-to-all | bytes 262144 | tf_op jit(solution)/shard_map/all_to_all | solution.py:100
  66.4 0.2 reshape.167
  66.6 0.1 bitcast_reduce_fusion.1
  66.7 0.2 multiply_reduce_fusion.2
  66.9 0.3 fusion.87
  67.3 0.7 fusion.82
  68.0 0.2 copy.83
  68.2 0.2 copy.82
  68.4 0.5 fusion.88
  68.9 0.3 fusion.90
  69.2 1.1 copy.81
  70.3 1.2 fusion.19
  71.4 1.2 copy.85
  72.7 1.1 fusion.46
  73.8 0.1 fusion.81
  73.9 0.2 multiply_reduce_fusion.1
  74.1 0.3 convolution_convert_fusion.1
  74.4 0.1 copy.86
  74.5 0.1 reshape.173
  74.7 39.3 %all-gather = bf16[32,4,2048]{2,1,0:T(4,128)(2,1)S(1)} all-gather(bf16[1,4,2048]{2,1,0:T(4,128)(2,1)S(1)} %reshape.173), channel_id=1, replica_groups=mesh['crop'=1,'res'=32] {'res'}, dimensions={0}, use_global_device_ids=true | all-gather | bytes 540672 | tf_op jit(solution)/shard_map/all_gather | solution.py:122
  114.0 1.2 reshape.160
  115.2 2.6 %copy.109 = bf16[128,64,32,1]{0,1,3,2:T(8,128)(2,1)S(1)} copy(bf16[128,64,32,1]{2,1,0,3:T(8,128)(2,1)S(1)} %bitcast.133) | data formatting | bytes 1048576 | tf_op jit(solution)/shard_map/reshape | solution.py:124
  117.8 0.4 fusion.6
  118.2 0.7 copy.88
  118.9 0.4 fusion.89
  119.4 0.3 convolution_bitcast_fusion
  119.7 0.1 fusion.25
  119.8 0.1 copy.97
  120.0 0.7 copy.98
  120.7 2.6 %all-to-all-start.2 = ((bf16[32,4,4,128]{3,1,2,0:T(4,128)(2,1)}), bf16[32,4,4,128]{3,1,2,0:T(4,128)(2,1)S(1)}, u32[]{:S(2)}, u32[]{:S(2)}) async-start(bf16[32,4,4,128]{3,1,2,0:T(4,128)(2,1)} %copy.98), calls=%async_computation.2 | async-start | bytes 262144 | tf_op jit(solution)/shard_map/all_to_all | solution.py:160
  123.3 0.1 copy.94
  123.4 0.7 copy.95
  124.1 7.4 %all-to-all-done.2 = bf16[32,4,4,128]{3,1,2,0:T(4,128)(2,1)S(1)} async-done(((bf16[32,4,4,128]{3,1,2,0:T(4,128)(2,1)}), bf16[32,4,4,128]{3,1,2,0:T(4,128)(2,1)S(1)}, u32[]{:S(2)}, u32[]{:S(2)}) %all-to-all-start.2) | async-done | bytes 131104 | tf_op jit(solution)/shard_map/all_to_all | solution.py:160
  131.5 2.6 %all-to-all-start.1 = ((bf16[32,4,4,128]{3,1,2,0:T(4,128)(2,1)}), bf16[32,4,4,128]{3,1,2,0:T(4,128)(2,1)S(1)}, u32[]{:S(2)}, u32[]{:S(2)}) async-start(bf16[32,4,4,128]{3,1,2,0:T(4,128)(2,1)} %copy.95), calls=%async_computation.1 | async-start | bytes 262144 | tf_op jit(solution)/shard_map/all_to_all | solution.py:159
  134.1 8.1 %all-to-all-done.1 = bf16[32,4,4,128]{3,1,2,0:T(4,128)(2,1)S(1)} async-done(((bf16[32,4,4,128]{3,1,2,0:T(4,128)(2,1)}), bf16[32,4,4,128]{3,1,2,0:T(4,128)(2,1)S(1)}, u32[]{:S(2)}, u32[]{:S(2)}) %all-to-all-start.1) | async-done | bytes 131104 | tf_op jit(solution)/shard_map/all_to_all | solution.py:159
  142.3 0.2 fusion.13
  142.5 0.8 copy.100
  143.3 2.6 %all-to-all-start.3 = ((bf16[1,4,128,128]{3,1,0,2:T(4,128)(2,1)}), bf16[1,4,128,128]{3,1,0,2:T(4,128)(2,1)S(1)}, u32[]{:S(2)}, u32[]{:S(2)}) async-start(bf16[1,4,128,128]{3,1,0,2:T(4,128)(2,1)} %copy.100), calls=%async_computation.3 | async-start | bytes 262144 | tf_op jit(solution)/shard_map/all_to_all | solution.py:163
  145.9 0.8 copy.104
  146.6 0.3 fusion.10
  146.9 7.2 %all-to-all-done.3 = bf16[1,4,128,128]{3,1,0,2:T(4,128)(2,1)S(1)} async-done(((bf16[1,4,128,128]{3,1,0,2:T(4,128)(2,1)}), bf16[1,4,128,128]{3,1,0,2:T(4,128)(2,1)S(1)}, u32[]{:S(2)}, u32[]{:S(2)}) %all-to-all-start.3) | async-done | bytes 131104 | tf_op jit(solution)/shard_map/all_to_all | solution.py:163
  154.2 0.1 fusion.44
  154.3 0.2 fusion.12
  154.6 0.8 copy.105
  (44 shorter events, 0.6 us)
Async XLA Ops:
  0.6 47.5 %copy-start = (bf16[256,1024]{1,0:T(8,128)(2,1)S(1)}, bf16[256,1024]{1,0:T(8,128)(2,1)}, u32[]{:S(2)}) copy-start(bf16[256,1024]{1,0:T(8,128)(2,1)} %param.20) | copy-start | bytes 1572868
  0.6 46.9 %copy-start.9 = (bf16[23,256]{1,0:T(8,128)(2,1)S(1)}, bf16[23,256]{1,0:T(8,128)(2,1)}, u32[]{:S(2)}) copy-start(bf16[23,256]{1,0:T(8,128)(2,1)} %param.18) | copy-start | bytes 35332
  0.7 46.9 %copy-start.5 = (bf16[2,128,256]{2,1,0:T(8,128)(2,1)S(1)}, bf16[2,128,256]{2,1,0:T(8,128)(2,1)}, u32[]{:S(2)}) copy-start(bf16[2,128,256]{2,1,0:T(8,128)(2,1)} %param.16) | copy-start | bytes 393220
  0.7 46.9 %copy-start.10 = (s32[2,128]{1,0:T(2,128)S(1)}, s32[2,128]{1,0:T(2,128)}, u32[]{:S(2)}) copy-start(s32[2,128]{1,0:T(2,128)} %param.14) | copy-start | bytes 3076
  49.3 0.6 copy-start.1
  49.5 0.7 copy-start.2
  54.0 12.9 %copy-start.3 = (bf16[256,1024]{1,0:T(8,128)(2,1)S(1)}, bf16[256,1024]{1,0:T(8,128)(2,1)}, u32[]{:S(2)}) copy-start(bf16[256,1024]{1,0:T(8,128)(2,1)} %param.22) | copy-start | bytes 1572868
  71.4 2.7 %copy-start.7 = (bf16[256,64]{0,1:T(8,128)(2,1)S(1)}, bf16[256,64]{0,1:T(8,128)(2,1)}, u32[]{:S(2)}) copy-start(bf16[256,64]{0,1:T(8,128)(2,1)} %param.24) | copy-start | bytes 98308
  117.8 1.1 copy-start.4
  118.2 1.1 copy-start.6
  120.7 10.8 %all-to-all-start.2 = ((bf16[32,4,4,128]{3,1,2,0:T(4,128)(2,1)}), bf16[32,4,4,128]{3,1,2,0:T(4,128)(2,1)S(1)}, u32[]{:S(2)}, u32[]{:S(2)}) async-start(bf16[32,4,4,128]{3,1,2,0:T(4,128)(2,1)} %copy.98), calls=%async_computation.2 | async-start | bytes 262144 | tf_op jit(solution)/shard_map/all_to_all | solution.py:160
  123.4 30.9 %copy-start.8 = (bf16[128,128]{1,0:T(8,128)(2,1)S(1)}, bf16[128,128]{1,0:T(8,128)(2,1)}, u32[]{:S(2)}) copy-start(bf16[128,128]{1,0:T(8,128)(2,1)} %param.27) | copy-start | bytes 98308
  131.5 10.8 %all-to-all-start.1 = ((bf16[32,4,4,128]{3,1,2,0:T(4,128)(2,1)}), bf16[32,4,4,128]{3,1,2,0:T(4,128)(2,1)S(1)}, u32[]{:S(2)}, u32[]{:S(2)}) async-start(bf16[32,4,4,128]{3,1,2,0:T(4,128)(2,1)} %copy.95), calls=%async_computation.1 | async-start | bytes 262144 | tf_op jit(solution)/shard_map/all_to_all | solution.py:159
  143.3 10.8 %all-to-all-start.3 = ((bf16[1,4,128,128]{3,1,0,2:T(4,128)(2,1)}), bf16[1,4,128,128]{3,1,0,2:T(4,128)(2,1)S(1)}, u32[]{:S(2)}, u32[]{:S(2)}) async-start(bf16[1,4,128,128]{3,1,0,2:T(4,128)(2,1)} %copy.100), calls=%async_computation.3 | async-start | bytes 262144 | tf_op jit(solution)/shard_map/all_to_all | solution.py:163
where the time goes:
time: 156 us; the launch traced here: 155 us
  blocking collectives  93.2 us (60%)
  waiting for transfers between devices  22.7 us (15%)
  local copies, waits for them, and re-layouts  17.4 us (11%)
  matrix products  11 us (7%)
  starting transfers between devices  7.73 us (5%)
  other arithmetic  2.2 us (1%)
    all_gather x1, blocking collectives, shards(): bias_all = lax.all_gather(bias_local, 'res', axis=1, tiled=True)  43.9 us
    all_gather x1, blocking collectives, shards(): piece = lax.all_gather(latter_factor, 'res', axis=0, tiled=True)  39.3 us
    all_to_all x1, blocking collectives, shards(): lax.all_to_all(alignment_after_rows, 'res', split_axis=1, concat_axis=0,...  9.91 us
    all_to_all x1, waiting for transfers between devices, shards(): lax.all_to_all(left_f, 'res', split_axis=0, concat_axis=2, tiled=True)  8.14 us
    all_to_all x1, waiting for transfers between devices, shards(): lax.all_to_all(right_f, 'res', split_axis=0, concat_axis=2, tiled=True)  7.35 us
    all_to_all x1, waiting for transfers between devices, shards(): lax.all_to_all(combined, 'res', split_axis=2, concat_axis=0, tiled=True)  7.17 us
    reshape x2, local copies, waits for them, and re-layouts, shards(): right_rows = piece.reshape(count, sequence_total, outer_chan)  3.78 us
    unnamed x26, local copies, waits for them, and re-layouts  3.38 us
  transfers between devices with their start and end apart: 3, of which 3 were waited for; matrix products, arithmetic and copies ran while one was open for 1% of the time, Pallas kernels for 0%

commit v1 on v0

--- a/solution.py
+++ b/solution.py
@@ -160,7 +160,10 @@
         lax.all_to_all(right_f, "res", split_axis=0, concat_axis=2, tiled=True),
         preferred_element_type=jnp.float32,
     ).astype(jnp.bfloat16)
-    back_rows = lax.all_to_all(combined, "res", split_axis=2, concat_axis=0, tiled=True)
+    back_rows = jnp.concatenate(
+        lax.all_to_all(jnp.stack(jnp.split(combined, lax.axis_size("res"), axis=2)), "res", 0, 0),
+        axis=0,
+    )
     back_rows = back_rows.reshape(pair_chan, res_local, chain_total)
     comb_normed = layer_normalized(back_rows.astype(jnp.float32), 0).astype(jnp.bfloat16)
     tri_update = jnp.einsum(

time: 156 us -> 175 us (1.12)
  local copies, waits for them, and re-layouts: 17.4 us -> 35.9 us
    unnamed x26 -> x57, local copies, waits for them, and re-layouts: 3.38 us -> 21.9 us
where the time goes in v1:
time: 175 us; the launch traced here: 174 us
  blocking collectives  93.2 us (53%)
  local copies, waits for them, and re-layouts  35.9 us (21%)
  waiting for transfers between devices  22.7 us (13%)
  matrix products  11.1 us (6%)
  starting transfers between devices  7.73 us (4%)
  other arithmetic  2.32 us (1%)
    all_gather x1, blocking collectives, shards(): bias_all = lax.all_gather(bias_local, 'res', axis=1, tiled=True)  43.9 us
    all_gather x1, blocking collectives, shards(): piece = lax.all_gather(latter_factor, 'res', axis=0, tiled=True)  39.3 us
    unnamed x57, local copies, waits for them, and re-layouts  21.9 us
    all_to_all x1, blocking collectives, shards(): lax.all_to_all(alignment_after_rows, 'res', split_axis=1, concat_axis=0,...  9.91 us
    all_to_all x1, waiting for transfers between devices, shards(): lax.all_to_all(left_f, 'res', split_axis=0, concat_axis=2, tiled=True)  8.14 us
    all_to_all x1, waiting for transfers between devices, shards(): lax.all_to_all(right_f, 'res', split_axis=0, concat_axis=2, tiled=True)  7.35 us
    all_to_all x1, waiting for transfers between devices, shards(): lax.all_to_all(jnp.stack(jnp.split(combined, lax.axis_size('res'), axis=2...  7.17 us
    reshape x2, local copies, waits for them, and re-layouts, shards(): right_rows = piece.reshape(count, sequence_total, outer_chan)  3.78 us
  transfers between devices with their start and end apart: 3, of which 3 were waited for; matrix products, arithmetic and copies ran while one was open for 1% of the time, Pallas kernels for 0%

profile of v1, /device:TPU:0, one launch (start us, length us, event | category | flops | bytes accessed | tf_op | source)
XLA Modules:
  0.0 174.1 jit_solution(11891882801990096274)
XLA Ops:
  0.7 0.7 add_multiply_fusion
  1.4 1.0 copy.73
  2.5 0.8 fusion.14
  3.4 43.9 %all_gather.6 = bf16[8,128,128]{2,0,1:T(8,128)(2,1)S(1)} all-gather(bf16[8,4,128]{2,0,1:T(8,128)(2,1)S(1)} %fusion.14), channel_id=1, replica_groups=mesh['crop'=1,'res'=32] {'res'}, dimensions={1}, use_global_device_ids=true | all-gather | bytes 270336 | tf_op jit(solution)/shard_map/all_gather | solution.py:94
  48.5 0.7 fusion.81
  50.1 0.5 fusion.84
  50.6 1.3 convolution_add_fusion
  51.9 1.0 copy.70
  53.0 1.0 fusion.20
  54.0 1.1 copy.77
  55.2 1.1 fusion.11
  56.4 9.9 %all_to_all.44 = bf16[2,128,256]{2,0,1:T(2,128)(2,1)S(1)} all-to-all(bf16[2,128,256]{2,0,1:T(2,128)(2,1)S(1)} %copy.78), channel_id=1, replica_groups=mesh['crop'=1,'res'=32] {'res'}, dimensions={1} | all-to-all | bytes 262144 | tf_op jit(solution)/shard_map/all_to_all | solution.py:100
  67.3 0.7 fusion.80
  68.4 0.5 fusion.86
  69.2 1.1 copy.80
  70.3 1.2 fusion.19
  71.4 1.2 copy.84
  72.7 1.1 fusion.44
  74.7 39.3 %all-gather = bf16[32,4,2048]{2,1,0:T(4,128)(2,1)S(1)} all-gather(bf16[1,4,2048]{2,1,0:T(4,128)(2,1)S(1)} %reshape.165), channel_id=1, replica_groups=mesh['crop'=1,'res'=32] {'res'}, dimensions={0}, use_global_device_ids=true | all-gather | bytes 540672 | tf_op jit(solution)/shard_map/all_gather | solution.py:122
  114.0 1.2 reshape.154
  115.2 2.6 %copy.106 = bf16[128,64,32,1]{0,1,3,2:T(8,128)(2,1)S(1)} copy(bf16[128,64,32,1]{2,1,0,3:T(8,128)(2,1)S(1)} %bitcast.252) | data formatting | bytes 1048576 | tf_op jit(solution)/shard_map/reshape | solution.py:124
  118.2 0.7 copy.87
  120.0 0.7 copy.97
  120.7 2.6 %all-to-all-start.2 = ((bf16[32,4,4,128]{3,1,2,0:T(4,128)(2,1)}), bf16[32,4,4,128]{3,1,2,0:T(4,128)(2,1)S(1)}, u32[]{:S(2)}, u32[]{:S(2)}) async-start(bf16[32,4,4,128]{3,1,2,0:T(4,128)(2,1)} %copy.97), calls=%async_computation.2 | async-start | bytes 262144 | tf_op jit(solution)/shard_map/all_to_all | solution.py:160
  123.4 0.7 copy.94
  124.1 7.4 %all-to-all-done.2 = bf16[32,4,4,128]{3,1,2,0:T(4,128)(2,1)S(1)} async-done(((bf16[32,4,4,128]{3,1,2,0:T(4,128)(2,1)}), bf16[32,4,4,128]{3,1,2,0:T(4,128)(2,1)S(1)}, u32[]{:S(2)}, u32[]{:S(2)}) %all-to-all-start.2) | async-done | bytes 131104 | tf_op jit(solution)/shard_map/all_to_all | solution.py:160
  131.5 2.6 %all-to-all-start.1 = ((bf16[32,4,4,128]{3,1,2,0:T(4,128)(2,1)}), bf16[32,4,4,128]{3,1,2,0:T(4,128)(2,1)S(1)}, u32[]{:S(2)}, u32[]{:S(2)}) async-start(bf16[32,4,4,128]{3,1,2,0:T(4,128)(2,1)} %copy.94), calls=%async_computation.1 | async-start | bytes 262144 | tf_op jit(solution)/shard_map/all_to_all | solution.py:159
  134.1 8.1 %all-to-all-done.1 = bf16[32,4,4,128]{3,1,2,0:T(4,128)(2,1)S(1)} async-done(((bf16[32,4,4,128]{3,1,2,0:T(4,128)(2,1)}), bf16[32,4,4,128]{3,1,2,0:T(4,128)(2,1)S(1)}, u32[]{:S(2)}, u32[]{:S(2)}) %all-to-all-start.1) | async-done | bytes 131104 | tf_op jit(solution)/shard_map/all_to_all | solution.py:159
  142.5 0.6 constant_dynamic-update-slice_fusion.31
  143.1 0.6 constant_dynamic-update-slice_fusion.30
  143.7 0.6 constant_dynamic-update-slice_fusion.29
  144.3 0.6 constant_dynamic-update-slice_fusion.28
  144.9 0.6 constant_dynamic-update-slice_fusion.27
  145.5 0.6 constant_dynamic-update-slice_fusion.26
  146.1 0.6 constant_dynamic-update-slice_fusion.25
  146.7 0.6 constant_dynamic-update-slice_fusion.24
  147.3 0.6 constant_dynamic-update-slice_fusion.23
  147.9 0.6 constant_dynamic-update-slice_fusion.22
  148.5 0.6 constant_dynamic-update-slice_fusion.21
  149.1 0.6 constant_dynamic-update-slice_fusion.20
  149.7 0.6 constant_dynamic-update-slice_fusion.19
  150.3 0.6 constant_dynamic-update-slice_fusion.18
  150.9 0.6 constant_dynamic-update-slice_fusion.17
  151.5 0.6 constant_dynamic-update-slice_fusion.16
  152.1 0.6 constant_dynamic-update-slice_fusion.15
  152.7 0.6 constant_dynamic-update-slice_fusion.14
  153.3 0.6 constant_dynamic-update-slice_fusion.13
  153.9 0.6 constant_dynamic-update-slice_fusion.12
  154.5 0.6 constant_dynamic-update-slice_fusion.11
  155.1 0.6 constant_dynamic-update-slice_fusion.10
  155.7 0.6 constant_dynamic-update-slice_fusion.9
  156.3 0.6 constant_dynamic-update-slice_fusion.8
  156.9 0.6 constant_dynamic-update-slice_fusion.7
  157.5 0.6 constant_dynamic-update-slice_fusion.6
  158.1 0.6 constant_dynamic-update-slice_fusion.5
  158.7 0.6 constant_dynamic-update-slice_fusion.4
  159.3 0.6 constant_dynamic-update-slice_fusion.3
  159.9 0.6 constant_dynamic-update-slice_fusion.2
  160.5 0.6 constant_dynamic-update-slice_fusion.1
  161.1 0.6 constant_dynamic-update-slice_fusion
  161.7 2.6 %all-to-all-start.3 = ((bf16[32,1,4,4,128]{4,3,2,1,0:T(4,128)(2,1)}), bf16[32,1,4,4,128]{4,3,2,1,0:T(4,128)(2,1)S(1)}, u32[]{:S(2)}, u32[]{:S(2)}) async-start(bf16[32,1,4,4,128]{4,3,2,1,0:T(4,128)(2,1)} %constant_dynamic-update-slice_fusion), calls=%async_computation.3 | async-start | bytes 262144 | tf_op jit(solution)/shard_map/all_to_all | solution.py:164
  164.3 0.8 copy.101
  165.3 7.2 %all-to-all-done.3 = bf16[32,1,4,4,128]{4,3,2,1,0:T(4,128)(2,1)S(1)} async-done(((bf16[32,1,4,4,128]{4,3,2,1,0:T(4,128)(2,1)}), bf16[32,1,4,4,128]{4,3,2,1,0:T(4,128)(2,1)S(1)}, u32[]{:S(2)}, u32[]{:S(2)}) %all-to-all-start.3) | async-done | bytes 131104 | tf_op jit(solution)/shard_map/all_to_all | solution.py:164
  173.3 0.8 copy.102
  (75 shorter events, 7.7 us)
Async XLA Ops:
  0.6 47.5 %copy-start = (bf16[256,1024]{1,0:T(8,128)(2,1)S(1)}, bf16[256,1024]{1,0:T(8,128)(2,1)}, u32[]{:S(2)}) copy-start(bf16[256,1024]{1,0:T(8,128)(2,1)} %param.20) | copy-start | bytes 1572868
  0.6 46.9 %copy-start.9 = (bf16[23,256]{1,0:T(8,128)(2,1)S(1)}, bf16[23,256]{1,0:T(8,128)(2,1)}, u32[]{:S(2)}) copy-start(bf16[23,256]{1,0:T(8,128)(2,1)} %param.18) | copy-start | bytes 35332
  0.7 46.9 %copy-start.5 = (bf16[2,128,256]{2,1,0:T(8,128)(2,1)S(1)}, bf16[2,128,256]{2,1,0:T(8,128)(2,1)}, u32[]{:S(2)}) copy-start(bf16[2,128,256]{2,1,0:T(8,128)(2,1)} %param.16) | copy-start | bytes 393220
  0.7 46.9 %copy-start.10 = (s32[2,128]{1,0:T(2,128)S(1)}, s32[2,128]{1,0:T(2,128)}, u32[]{:S(2)}) copy-start(s32[2,128]{1,0:T(2,128)} %param.14) | copy-start | bytes 3076
  49.3 0.6 copy-start.1
  49.5 0.7 copy-start.2
  54.0 12.9 %copy-start.3 = (bf16[256,1024]{1,0:T(8,128)(2,1)S(1)}, bf16[256,1024]{1,0:T(8,128)(2,1)}, u32[]{:S(2)}) copy-start(bf16[256,1024]{1,0:T(8,128)(2,1)} %param.22) | copy-start | bytes 1572868
  71.4 2.7 %copy-start.7 = (bf16[256,64]{0,1:T(8,128)(2,1)S(1)}, bf16[256,64]{0,1:T(8,128)(2,1)}, u32[]{:S(2)}) copy-start(bf16[256,64]{0,1:T(8,128)(2,1)} %param.24) | copy-start | bytes 98308
  117.8 1.1 copy-start.4
  118.2 1.1 copy-start.6
  120.7 10.8 %all-to-all-start.2 = ((bf16[32,4,4,128]{3,1,2,0:T(4,128)(2,1)}), bf16[32,4,4,128]{3,1,2,0:T(4,128)(2,1)S(1)}, u32[]{:S(2)}, u32[]{:S(2)}) async-start(bf16[32,4,4,128]{3,1,2,0:T(4,128)(2,1)} %copy.97), calls=%async_computation.2 | async-start | bytes 262144 | tf_op jit(solution)/shard_map/all_to_all | solution.py:160
  123.4 49.5 %copy-start.8 = (bf16[128,128]{1,0:T(8,128)(2,1)S(1)}, bf16[128,128]{1,0:T(8,128)(2,1)}, u32[]{:S(2)}) copy-start(bf16[128,128]{1,0:T(8,128)(2,1)} %param.27) | copy-start | bytes 98308
  131.5 10.8 %all-to-all-start.1 = ((bf16[32,4,4,128]{3,1,2,0:T(4,128)(2,1)}), bf16[32,4,4,128]{3,1,2,0:T(4,128)(2,1)S(1)}, u32[]{:S(2)}, u32[]{:S(2)}) async-start(bf16[32,4,4,128]{3,1,2,0:T(4,128)(2,1)} %copy.94), calls=%async_computation.1 | async-start | bytes 262144 | tf_op jit(solution)/shard_map/all_to_all | solution.py:159
  161.7 10.8 %all-to-all-start.3 = ((bf16[32,1,4,4,128]{4,3,2,1,0:T(4,128)(2,1)}), bf16[32,1,4,4,128]{4,3,2,1,0:T(4,128)(2,1)S(1)}, u32[]{:S(2)}, u32[]{:S(2)}) async-start(bf16[32,1,4,4,128]{4,3,2,1,0:T(4,128)(2,1)} %constant_dynamic-update-slice_fusion), calls=%async_computation.3 | async-start | bytes 262144 | tf_op jit(solution)/shard_map/all_to_all | solution.py:164
